TPU v7x, 256 devices: a whole 4x4x8 slice. The times are simulated.
256 devices in a mesh: subj: 8 (over x, core), space: 32 (over y, z).
Axes of the slice: x: 4, y: 4, z: 8, core: 2. Of those that a mesh axis runs over, the one named last changes fastest.
Arguments:
- images: bfloat16 [16, 2048, 16, 128], P('subj', 'space'), may hold values from -6 to 6
- velocity: float32 [3, 16, 2048, 16, 128], P(None, 'subj', 'space'), may hold values from -4 to 4
- weights: bfloat16 [3, 16, 2048, 16, 128], P(None, 'subj', 'space'), may hold values from 0 to 1
- template: float32 [2048, 16, 128], P('space', 'subj'), may hold values from -6 to 6
- owners: int32 [16, 2048, 1], P('subj', 'space'), may hold values from 0 to 31; in each aligned block of 64 rows (0 to 63, 64 to 127, ..., all dimensions but the last counted through in order) at most 4 rows name the same one
- local_rows: int32 [16, 2048], P('subj', 'space'), may hold values from 0 to 63
- tile_counts: int32 [16, 32], P('subj', 'space'), may hold values from 32 to 64
Outputs:
- new_velocity: float32 [3, 16, 2048, 16, 128], P(None, 'subj', 'space')
- new_template: float32 [2048, 16, 128], P('space', 'subj')
Inputs may be any that keep to these rules, and one draw needn't show every extreme that they name: `owners`: for each subject and each aligned block of 64 tiles, no value appears more than 4 times, and some value appears exactly 4 times.
All inputs are finite; a program needn't handle non-finite values.
Results may differ from a plain program's by a relative error of at most 0.0006.
Values may be sent and summed in bfloat16 or wider, within the bound.
A program may use at most 64 MiB of HBM per device.

v0:
```python
import jax
import jax.numpy as jnp
from jax import lax
from jax.sharding import PartitionSpec as P

BX = 4
BY = 4
ITERS = 2
ridge = 0.25


def extended(block, sides, width):
    for axis, dim in sides:
        count = lax.axis_size(axis)
        forward = [(i, i + 1) for i in range(count - 1)]
        backward = [(target, source) for source, target in forward]
        low = lax.ppermute(
            lax.slice_in_dim(block, block.shape[dim] - width, None, axis=dim), axis, forward
        )
        high = lax.ppermute(lax.slice_in_dim(block, 0, width, axis=dim), axis, backward)
        block = jnp.concatenate([low, block, high], axis=dim)
    return block


def shift_up(field, axis):
    body_part = lax.slice_in_dim(field, 1, field.shape[axis], axis=axis)
    edge = jnp.zeros_like(lax.slice_in_dim(field, 0, 1, axis=axis))
    return jnp.concatenate([body_part, edge], axis)


def shift_down(field, axis):
    body_part = lax.slice_in_dim(field, 0, field.shape[axis] - 1, axis=axis)
    edge = jnp.zeros_like(lax.slice_in_dim(field, 0, 1, axis=axis))
    return jnp.concatenate([edge, body_part], axis)


def trilinear(brick, frac_x, frac_y, frac_z):
    depth = brick.ndim
    total = jnp.zeros_like(brick)
    for offset_x in (0, 1):
        moved_x = brick if offset_x == 0 else shift_up(brick, depth - 3)
        weight_x = 1.0 - frac_x if offset_x == 0 else frac_x
        for offset_y in (0, 1):
            moved = moved_x if offset_y == 0 else shift_up(moved_x, depth - 2)
            weight_y = 1.0 - frac_y if offset_y == 0 else frac_y
            along_z = (1.0 - frac_z) * moved + frac_z * shift_up(moved, depth - 1)
            total = total + weight_x * weight_y * along_z
    return total


def gradients(field):
    depth = field.ndim
    return jnp.stack(
        [
            0.5 * (shift_up(field, depth - 3 + offset) - shift_down(field, depth - 3 + offset))
            for offset in range(3)
        ]
    )


def smooth_z(field):
    depth = field.ndim
    return 0.25 * shift_down(field, depth - 1) + 0.5 * field + 0.25 * shift_up(field, depth - 1)


def predict(warped, grads, field):
    return warped + (grads[0] * field[0] + grads[1] * field[1]) + grads[2] * field[2]


def body(images, velocity, weights, template, owners, local_rows, tile_counts):
    spaces = lax.axis_size("space")
    groups = lax.axis_size("subj")
    subj_dev = images.shape[0]
    rows_dev = images.shape[1]
    plane = images.shape[2]
    depth_z = images.shape[3]
    cap = 2 * rows_dev // spaces
    subjects = subj_dev * groups
    position = jnp.arange(rows_dev, dtype=jnp.int32)[None, :]
    first = tile_counts // 2
    alive = (position < first) | (position >= rows_dev - (tile_counts - first))
    owner = owners[:, :, 0]
    hits = (owner[:, :, None] == jnp.arange(spaces, dtype=jnp.int32)[None, None, :]).astype(
        jnp.int32
    )
    hits = hits * alive.astype(jnp.int32)[:, :, None]
    before = jnp.cumsum(hits, axis=1) - hits
    place = jnp.sum(before * hits, axis=2)
    slot = jnp.where(alive, owner * cap + place, spaces * cap)
    request = jnp.zeros((subj_dev, spaces * cap), jnp.int32)
    request = request.at[jnp.arange(subj_dev)[:, None], slot].set(local_rows, mode="drop")
    request = request.reshape(subj_dev, spaces, cap)
    wanted = lax.all_to_all(request, "space", split_axis=1, concat_axis=1, tiled=True)
    returned = lax.all_to_all(
        jax.vmap(lambda image, index: image[index])(images, wanted),
        "space",
        split_axis=1,
        concat_axis=1,
        tiled=True,
    )
    returned = returned.reshape(subj_dev, spaces * cap, plane, depth_z)
    read_slot = jnp.minimum(slot, spaces * cap - 1)
    fetched = jax.vmap(lambda table, index: table[index])(returned, read_slot)
    live = alive.astype(jnp.float32)
    brick = fetched.astype(jnp.float32).reshape(subj_dev, rows_dev, BX, BY, depth_z)
    frac = weights.astype(jnp.float32).reshape(3, subj_dev, rows_dev, BX, BY, depth_z)
    warped = trilinear(brick, frac[0], frac[1], frac[2]) * live[:, :, None, None, None]
    grads = gradients(warped)
    whole = lax.all_gather(template, "subj", axis=1, tiled=True)
    current = whole.reshape(rows_dev, BX, BY, depth_z)
    field = velocity.reshape(3, subj_dev, rows_dev, BX, BY, depth_z)
    piece = plane // groups
    result = template
    for step in range(ITERS):
        predicted = predict(warped, grads, field)
        ratio = (predicted - current[None]) / (
            grads[0] * grads[0] + grads[1] * grads[1] + grads[2] * grads[2] + ridge
        )
        update = grads * ratio[None]
        padded = extended(update, (("space", 2),), 1)
        rowwise = 0.25 * padded[:, :, :-2] + 0.5 * update + 0.25 * padded[:, :, 2:]
        field = field - smooth_z(rowwise)
        local_sum = jnp.sum(predict(warped, grads, field), axis=0).reshape(rows_dev, plane, depth_z)
        total = lax.psum(local_sum, "subj") / subjects
        current = total.reshape(rows_dev, BX, BY, depth_z)
        result = lax.dynamic_slice_in_dim(total, lax.axis_index("subj") * piece, piece, 1)
    return (field.reshape(3, subj_dev, rows_dev, plane, depth_z), result)


def solution(mesh):
    in_specs = (
        P("subj", "space", None, None),
        P(None, "subj", "space", None, None),
        P(None, "subj", "space", None, None),
        P("space", "subj", None),
        P("subj", "space", None),
        P("subj", "space"),
        P("subj", "space"),
    )
    out_specs = (P(None, "subj", "space", None, None), P("space", "subj", None))
    return jax.shard_map(body, mesh=mesh, in_specs=in_specs, out_specs=out_specs, check_vma=False)
```

profile of v0, /device:TPU:8, one launch (start us, length us, event | category | flops | bytes accessed | tf_op | source)
XLA Modules:
  0.0 271.9 jit_solution(7685412767636631632)
XLA Ops:
  11.4 6.4 %scatter_fusion = s32[2,128]{1,0:T(2,128)S(1)} fusion(s32[2,128]{1,0:T(2,128)S(1)} %broadcast_in_dim.10, s32[128]{0:T(128)S(1)} %reshape.240, s32[128]{0:T(128)S(1)} %reshape.242), kind=kCustom, calls=%fused_computation.2 | custom fusion | bytes 2560 | tf_op jit(solution)/shard_map/scatter | solution.py:91
  17.9 20.2 %all_to_all.10 = s32[2,32,4]{2,0,1:T(2,128)S(1)} all-to-all(s32[2,32,4]{2,0,1:T(2,128)S(1)} %copy.24), channel_id=1, replica_groups=mesh['subj'=8,'space'=32] {'space'}, dimensions={1} | all-to-all | bytes 2048 | tf_op jit(solution)/shard_map/all_to_all | solution.py:93
  38.4 1.2 gather_fusion
  39.7 1.1 copy.29
  40.8 5.8 %all-to-all-start.1 = ((bf16[2,32,4,16,128]{4,3,2,0,1:T(8,128)(2,1)}), bf16[2,32,4,16,128]{4,3,2,0,1:T(8,128)(2,1)}, u32[]{:S(2)}, u32[]{:S(2)}) async-start(bf16[2,32,4,16,128]{4,3,2,0,1:T(8,128)(2,1)} %copy.29), calls=%async_computation.1 | async-start | bytes 2097152 | tf_op jit(solution)/shard_map/all_to_all | solution.py:94
  46.8 13.5 %all_gather.3 = f32[64,16,128]{2,0,1:T(8,128)S(1)} all-gather(f32[64,2,128]{2,0,1:T(8,128)S(1)} %copy.31), channel_id=1, replica_groups=mesh['subj'=8,'space'=32] {'subj'}, dimensions={1}, use_global_device_ids=true | all-gather | bytes 589824 | tf_op jit(solution)/shard_map/all_gather | solution.py:109
  60.2 1.2 copy.32
  61.4 1.6 fusion.52
  64.0 1.7 fusion.51
  65.8 5.9 %all-to-all-done.1 = bf16[2,32,4,16,128]{4,3,2,0,1:T(8,128)(2,1)} async-done(((bf16[2,32,4,16,128]{4,3,2,0,1:T(8,128)(2,1)}), bf16[2,32,4,16,128]{4,3,2,0,1:T(8,128)(2,1)}, u32[]{:S(2)}, u32[]{:S(2)}) %all-to-all-start.1) | async-done | bytes 1048608 | tf_op jit(solution)/shard_map/all_to_all | solution.py:94
  71.7 1.4 copy.30
  76.7 2.3 fusion.12
  81.9 1.9 subtract_divide_fusion.1
  84.9 5.0 %collective-permute-start = (f32[3,2,1,4,4,128]{5,4,3,2,1,0:T(4,128)S(1)}, f32[3,2,1,4,4,128]{5,4,3,2,1,0:T(4,128)S(1)}, u32[]{:S(2)}, u32[]{:S(2)}) collective-permute-start(f32[3,2,1,4,4,128]{5,4,3,2,1,0:T(4,128)S(1)} %get-tuple-element.17), channel_id=1, source_target_pairs={{0,1},{1,2},{2,3},{3,4},{4,5},{5,6},{6,7},{7,8},{8,9},{9,10},{10,1... | collective-permute-start | bytes 147464 | tf_op jit(solution)/shard_map/ppermute | solution.py:17
  89.9 3.1 %collective-permute-start.1 = (f32[3,2,1,4,4,128]{5,4,3,2,1,0:T(4,128)S(1)}, f32[3,2,1,4,4,128]{5,4,3,2,1,0:T(4,128)S(1)}, u32[]{:S(2)}, u32[]{:S(2)}) collective-permute-start(f32[3,2,1,4,4,128]{5,4,3,2,1,0:T(4,128)S(1)} %get-tuple-element.18), channel_id=1, source_target_pairs={{1,0},{2,1},{3,2},{4,3},{5,4},{6,5},{7,6},{8,7},{9,8},{10,9},{11,1... | collective-permute-start | bytes 147464 | tf_op jit(solution)/shard_map/ppermute | solution.py:20
  93.1 2.9 %collective-permute-done.1 = f32[3,2,1,4,4,128]{5,4,3,2,1,0:T(4,128)S(1)} collective-permute-done((f32[3,2,1,4,4,128]{5,4,3,2,1,0:T(4,128)S(1)}, f32[3,2,1,4,4,128]{5,4,3,2,1,0:T(4,128)S(1)}, u32[]{:S(2)}, u32[]{:S(2)}) %collective-permute-start.1) | collective-permute-done | bytes 49184 | tf_op jit(solution)/shard_map/ppermute | solution.py:20
  95.9 2.2 fusion.5
  98.2 2.1 fusion.49
  100.3 4.2 %add_subtract_fusion.1 = f32[3,2,64,4,4,128]{5,4,3,2,1,0:T(4,128)S(1)} fusion(f32[3,2,64,4,4,128]{5,4,3,2,1,0:T(4,128)S(1)} %bitcast.99, f32[3,2,64,4,4,127]{5,4,3,2,1,0:T(4,128)S(1)} %get-tuple-element.16, f32[3,2,64,4,4,127]{5,4,3,2,1,0:T(4,128)S(1)} %get-tuple-element.15, f32[3,2,1,4,4,128]{5,4,3,2,1,0:T(4,128)S(1)} %collective-permute-done.1, ...), kind=kLoop, calls=%fused_computation.17 | loop fusion | flops 10223616 | bytes 15777792 | tf_op jit(solution)/shard_map/sub | solution.py:122
  104.5 3.3 %fusion.45 = (f32[64,4,4,128]{3,2,1,0:T(4,128)}, f32[2,64,4,4,128]{4,3,2,1,0:T(4,128)}) fusion(f32[2,64,4,4,128]{4,3,2,1,0:T(4,128)S(1)} %get-tuple-element.6, f32[3,2,64,4,4,128]{5,4,3,2,1,0:T(4,128)S(1)} %add_subtract_fusion.1, f32[2,64,4,4,128]{4,3,2,1,0:T(4,128)S(1)} %fusion.12, f32[2,64,4,4,128]{4,3,2,1,0:T(4,128)S(1)} %get-tuple-element.5, ...), kind=kLoop, calls=%fused_computation.94 | loop fusion | flops 2228224 | bytes 9437184 | tf_op jit(solution)/shard_map/reduce_sum | solution.py:123
  107.9 65.1 %all-reduce.20.cloned.1.call-done = f32[64,16,128]{2,1,0:T(8,128)} async-done(((f32[64,16,128]{2,1,0:T(8,128)}), f32[64,16,128]{2,1,0:T(8,128)}) %all-reduce.20.cloned.1.call-update) | async-done | bytes 524304 | tf_op jit(solution)/shard_map/psum | solution.py:124
  173.0 1.1 broadcast_multiply_fusion.2
  174.1 2.6 subtract_divide_fusion
  177.7 3.5 %collective-permute-start.2 = (f32[3,2,1,4,4,128]{5,4,3,2,1,0:T(4,128)S(1)}, f32[3,2,1,4,4,128]{5,4,3,2,1,0:T(4,128)S(1)}, u32[]{:S(2)}, u32[]{:S(2)}) collective-permute-start(f32[3,2,1,4,4,128]{5,4,3,2,1,0:T(4,128)S(1)} %get-tuple-element.13), channel_id=1, source_target_pairs={{0,1},{1,2},{2,3},{3,4},{4,5},{5,6},{6,7},{7,8},{8,9},{9,10},{10,1... | collective-permute-start | bytes 147464 | tf_op jit(solution)/shard_map/ppermute | solution.py:17
  181.1 4.7 %collective-permute-start.3 = (f32[3,2,1,4,4,128]{5,4,3,2,1,0:T(4,128)S(1)}, f32[3,2,1,4,4,128]{5,4,3,2,1,0:T(4,128)S(1)}, u32[]{:S(2)}, u32[]{:S(2)}) collective-permute-start(f32[3,2,1,4,4,128]{5,4,3,2,1,0:T(4,128)S(1)} %get-tuple-element.14), channel_id=1, source_target_pairs={{1,0},{2,1},{3,2},{4,3},{5,4},{6,5},{7,6},{8,7},{9,8},{10,9},{11,1... | collective-permute-start | bytes 147464 | tf_op jit(solution)/shard_map/ppermute | solution.py:20
  185.9 1.5 collective-permute-done.3
  187.4 2.2 fusion.1
  189.6 2.1 fusion.47
  191.8 4.2 %add_subtract_fusion = f32[3,2,64,4,4,128]{5,4,3,2,1,0:T(4,128)S(1)} fusion(f32[3,2,64,4,4,128]{5,4,3,2,1,0:T(4,128)S(1)} %copy-done.5, f32[3,2,64,4,4,127]{5,4,3,2,1,0:T(4,128)S(1)} %get-tuple-element.12, f32[3,2,64,4,4,127]{5,4,3,2,1,0:T(4,128)S(1)} %get-tuple-element.11, f32[3,2,1,4,4,128]{5,4,3,2,1,0:T(4,128)S(1)} %collective-permute-done.3, ...), kind=kLoop, calls=%fused_computation.16 | loop fusion | flops 10223616 | bytes 15777792 | tf_op jit(solution)/shard_map/sub | solution.py:122
  196.0 2.3 fusion.15
  198.4 65.1 %all-reduce.22.cloned.1.call-done = f32[64,16,128]{2,1,0:T(8,128)} async-done(((f32[64,16,128]{2,1,0:T(8,128)}), f32[64,16,128]{2,1,0:T(8,128)}) %all-reduce.22.cloned.1.call-update) | async-done | bytes 524304 | tf_op jit(solution)/shard_map/psum | solution.py:124
  263.4 1.6 dynamic-slice_multiply_fusion
  (80 shorter events, 14.2 us)
Async XLA Ops:
  7.2 31.3 %copy-start = (bf16[2,64,16,128]{3,2,1,0:T(8,128)(2,1)S(1)}, bf16[2,64,16,128]{3,2,1,0:T(8,128)(2,1)}, u32[]{:S(2)}) copy-start(bf16[2,64,16,128]{3,2,1,0:T(8,128)(2,1)} %param.7) | copy-start | bytes 1572868
  38.4 8.3 %copy-start.20 = (f32[64,2,128]{2,1,0:T(2,128)S(1)}, f32[64,2,128]{2,1,0:T(2,128)}, u32[]{:S(2)}) copy-start(f32[64,2,128]{2,1,0:T(2,128)} %param.10) | copy-start | bytes 196612
  39.7 21.7 %copy-start.13 = (bf16[3,2,64,16,128]{4,3,2,1,0:T(8,128)(2,1)S(1)}, bf16[3,2,64,16,128]{4,3,2,1,0:T(8,128)(2,1)}, u32[]{:S(2)}) copy-start(bf16[3,2,64,16,128]{4,3,2,1,0:T(8,128)(2,1)} %param.9) | copy-start | bytes 4718596
  40.8 30.8 %all-to-all-start.1 = ((bf16[2,32,4,16,128]{4,3,2,0,1:T(8,128)(2,1)}), bf16[2,32,4,16,128]{4,3,2,0,1:T(8,128)(2,1)}, u32[]{:S(2)}, u32[]{:S(2)}) async-start(bf16[2,32,4,16,128]{4,3,2,0,1:T(8,128)(2,1)} %copy.29), calls=%async_computation.1 | async-start | bytes 2097152 | tf_op jit(solution)/shard_map/all_to_all | solution.py:94
  46.6 126.4 %all-reduce.20.cloned.1.call-start = ((), (), s32[]{:S(2)}) async-start(), calls=%async_computation.2 | async-start | bytes 1048576 | tf_op jit(solution)/shard_map/psum | solution.py:124
  61.4 2.6 copy-start.8
  75.0 1.6 copy-start.17
  75.0 1.6 copy-start.18
  79.6 1.2 copy-start.14
  79.7 1.5 copy-start.15
  79.7 2.1 copy-start.16
  79.7 2.2 copy-start.19
  80.4 24.1 %copy-start.6 = (f32[2,64,3,4,128]{4,3,2,1,0:T(4,128)}, f32[2,64,3,4,128]{4,3,2,1,0:T(4,128)S(1)}, u32[]{:S(2)}) copy-start(f32[2,64,3,4,128]{4,3,2,1,0:T(4,128)S(1)} %get-tuple-element.31) | copy-start | bytes 2359300
  83.9 1.0 copy-start.11
  83.9 20.6 %copy-start.2 = (f32[2,64,4,4,128]{4,3,2,1,0:T(4,128)}, f32[2,64,4,4,128]{4,3,2,1,0:T(4,128)S(1)}, u32[]{:S(2)}) copy-start(f32[2,64,4,4,128]{4,3,2,1,0:T(4,128)S(1)} %get-tuple-element.6) | copy-start | bytes 3145732
  84.9 8.1 %collective-permute-start = (f32[3,2,1,4,4,128]{5,4,3,2,1,0:T(4,128)S(1)}, f32[3,2,1,4,4,128]{5,4,3,2,1,0:T(4,128)S(1)}, u32[]{:S(2)}, u32[]{:S(2)}) collective-permute-start(f32[3,2,1,4,4,128]{5,4,3,2,1,0:T(4,128)S(1)} %get-tuple-element.17), channel_id=1, source_target_pairs={{0,1},{1,2},{2,3},{3,4},{4,5},{5,6},{6,7},{7,8},{8,9},{9,10},{10,1... | collective-permute-start | bytes 147464 | tf_op jit(solution)/shard_map/ppermute | solution.py:17
  89.9 6.0 %collective-permute-start.1 = (f32[3,2,1,4,4,128]{5,4,3,2,1,0:T(4,128)S(1)}, f32[3,2,1,4,4,128]{5,4,3,2,1,0:T(4,128)S(1)}, u32[]{:S(2)}, u32[]{:S(2)}) collective-permute-start(f32[3,2,1,4,4,128]{5,4,3,2,1,0:T(4,128)S(1)} %get-tuple-element.18), channel_id=1, source_target_pairs={{1,0},{2,1},{3,2},{4,3},{5,4},{6,5},{7,6},{8,7},{9,8},{10,9},{11,1... | collective-permute-start | bytes 147464 | tf_op jit(solution)/shard_map/ppermute | solution.py:20
  98.2 2.2 copy-start.9
  104.5 3.3 %copy-start.4 = (f32[3,2,64,4,4,128]{5,4,3,2,1,0:T(4,128)}, f32[3,2,64,4,4,128]{5,4,3,2,1,0:T(4,128)S(1)}, u32[]{:S(2)}) copy-start(f32[3,2,64,4,4,128]{5,4,3,2,1,0:T(4,128)S(1)} %add_subtract_fusion.1) | copy-start | bytes 9437188
  107.9 155.5 %all-reduce.22.cloned.1.call-start = ((), (), s32[]{:S(2)}) async-start(), calls=%async_computation.3 | async-start | bytes 1048576 | tf_op jit(solution)/shard_map/psum | solution.py:124
  174.1 2.7 copy-start.3
  174.1 2.7 copy-start.12
  177.7 8.2 %collective-permute-start.2 = (f32[3,2,1,4,4,128]{5,4,3,2,1,0:T(4,128)S(1)}, f32[3,2,1,4,4,128]{5,4,3,2,1,0:T(4,128)S(1)}, u32[]{:S(2)}, u32[]{:S(2)}) collective-permute-start(f32[3,2,1,4,4,128]{5,4,3,2,1,0:T(4,128)S(1)} %get-tuple-element.13), channel_id=1, source_target_pairs={{0,1},{1,2},{2,3},{3,4},{4,5},{5,6},{6,7},{7,8},{8,9},{9,10},{10,1... | collective-permute-start | bytes 147464 | tf_op jit(solution)/shard_map/ppermute | solution.py:17
  181.1 6.2 %collective-permute-start.3 = (f32[3,2,1,4,4,128]{5,4,3,2,1,0:T(4,128)S(1)}, f32[3,2,1,4,4,128]{5,4,3,2,1,0:T(4,128)S(1)}, u32[]{:S(2)}, u32[]{:S(2)}) collective-permute-start(f32[3,2,1,4,4,128]{5,4,3,2,1,0:T(4,128)S(1)} %get-tuple-element.14), channel_id=1, source_target_pairs={{1,0},{2,1},{3,2},{4,3},{5,4},{6,5},{7,6},{8,7},{9,8},{10,9},{11,1... | collective-permute-start | bytes 147464 | tf_op jit(solution)/shard_map/ppermute | solution.py:20
  189.6 2.2 copy-start.5
  191.8 4.2 %copy-start.7 = (f32[2,64,3,4,128]{4,3,2,1,0:T(4,128)S(1)}, f32[2,64,3,4,128]{4,3,2,1,0:T(4,128)}, u32[]{:S(2)}) copy-start(f32[2,64,3,4,128]{4,3,2,1,0:T(4,128)} %copy-done.6) | copy-start | bytes 2359300
  191.8 73.2 %copy-start.1 = (bf16[2,64,16,128]{3,2,1,0:T(8,128)(2,1)S(1)}, bf16[2,64,16,128]{3,2,1,0:T(8,128)(2,1)}, u32[]{:S(2)}) copy-start(bf16[2,64,16,128]{3,2,1,0:T(8,128)(2,1)} %param.7) | copy-start | bytes 1572868
  196.0 2.3 copy-start.10
Sparse Core Ops, SparseCore 0:
  108.0 64.9 all-reduce.19
  198.5 64.9 all-reduce.21
where the time goes:
time: 272 us
  waiting for transfers between devices  140 us (51%)
  blocking collectives  33.6 us (12%)
  other arithmetic  33.1 us (12%)
  local copies, waits for them, and re-layouts  28 us (10%)
  starting transfers between devices  22.2 us (8%)
  between operations  14.5 us (5%)
    psum x2, waiting for transfers between devices, body(): total = lax.psum(local_sum, 'subj') / subjects  130 us
    all_to_all x1, blocking collectives, body(): lax.all_to_all(request, 'space', split_axis=1, concat_axis=1, tiled=True)  20.2 us
    all_gather x1, blocking collectives, body(): whole = lax.all_gather(template, 'subj', axis=1, tiled=True)  13.5 us
    ppermute x2, starting transfers between devices, extended(): lax.ppermute(lax.slice_in_dim(block, block.shape[dim] - width, None, axis...  8.5 us
    sub x2, other arithmetic, body(): field = field - smooth_z(rowwise)  8.33 us
    ppermute x2, starting transfers between devices, extended(): lax.ppermute(lax.slice_in_dim(block, 0, width, axis=dim), axis, backward)  7.8 us
    scatter x1, local copies, waits for them, and re-layouts, body(): request.at[jnp.arange(subj_dev)[:, None], slot].set(local_rows, mode='drop')  6.43 us
    all_to_all x1, waiting for transfers between devices, body(): lax.all_to_all(jax.vmap(lambda image, index: image[index])(images, wanted...  5.92 us
  transfers between devices with their start and end apart: 7, of which 5 were waited for; matrix products, arithmetic and copies ran while one was open for 2% of the time, Pallas kernels for 0%

commit v1 on v0

--- a/solution.py
+++ b/solution.py
@@ -121,7 +121,10 @@
         rowwise = 0.25 * padded[:, :, :-2] + 0.5 * update + 0.25 * padded[:, :, 2:]
         field = field - smooth_z(rowwise)
         local_sum = jnp.sum(predict(warped, grads, field), axis=0).reshape(rows_dev, plane, depth_z)
-        total = lax.psum(local_sum, "subj") / subjects
+        point_the_column = lambda x_local, mesh_ax: jnp.sum(
+            jax.lax.all_gather(x_local, mesh_ax), axis=0
+        )
+        total = point_the_column(local_sum, mesh_ax="subj") / subjects
         current = total.reshape(rows_dev, BX, BY, depth_z)
         result = lax.dynamic_slice_in_dim(total, lax.axis_index("subj") * piece, piece, 1)
     return (field.reshape(3, subj_dev, rows_dev, plane, depth_z), result)

time: 272 us -> 217 us (0.80)
  waiting for transfers between devices: 140 us -> 78.5 us
  other arithmetic: 33.1 us -> 38 us
    psum x2 -> x0, waiting for transfers between devices: 130 us -> none  [body(): total = lax.psum(local_sum, 'subj') / subjects]
    all_gather x0 -> x2, waiting for transfers between devices: none -> 68.2 us  [body(): jax.lax.all_gather(x_local, mesh_ax)]
    reduce_sum x0 -> x2, other arithmetic: none -> 5.85 us  [body(): jnp.sum(jax.lax.all_gather(x_local, mesh_ax), axis=0)]
where the time goes in v1:
time: 217 us; the launch traced here: 215 us
  waiting for transfers between devices  78.5 us (36%)
  other arithmetic  38 us (18%)
  blocking collectives  33.6 us (15%)
  local copies, waits for them, and re-layouts  28.1 us (13%)
  starting transfers between devices  22.2 us (10%)
  between operations  14.5 us (7%)
    all_gather x2, waiting for transfers between devices, body(): jax.lax.all_gather(x_local, mesh_ax)  68.2 us
    all_to_all x1, blocking collectives, body(): lax.all_to_all(request, 'space', split_axis=1, concat_axis=1, tiled=True)  20.2 us
    all_gather x1, blocking collectives, body(): whole = lax.all_gather(template, 'subj', axis=1, tiled=True)  13.5 us
    ppermute x2, starting transfers between devices, extended(): lax.ppermute(lax.slice_in_dim(block, block.shape[dim] - width, None, axis...  8.49 us
    sub x2, other arithmetic, body(): field = field - smooth_z(rowwise)  8.33 us
    ppermute x2, starting transfers between devices, extended(): lax.ppermute(lax.slice_in_dim(block, 0, width, axis=dim), axis, backward)  7.81 us
    scatter x1, local copies, waits for them, and re-layouts, body(): request.at[jnp.arange(subj_dev)[:, None], slot].set(local_rows, mode='drop')  6.43 us
    all_to_all x1, waiting for transfers between devices, body(): lax.all_to_all(jax.vmap(lambda image, index: image[index])(images, wanted...  5.92 us
  transfers between devices with their start and end apart: 7, of which 5 were waited for; matrix products, arithmetic and copies ran while one was open for 2% of the time, Pallas kernels for 0%

profile of v1, /device:TPU:8, one launch (start us, length us, event | category | flops | bytes accessed | tf_op | source)
XLA Modules:
  0.0 214.9 jit_solution(1506527320408840879)
XLA Ops:
  11.4 6.4 %scatter_fusion = s32[2,128]{1,0:T(2,128)S(1)} fusion(s32[2,128]{1,0:T(2,128)S(1)} %broadcast_in_dim.10, s32[128]{0:T(128)S(1)} %reshape.238, s32[128]{0:T(128)S(1)} %reshape.240), kind=kCustom, calls=%fused_computation.2 | custom fusion | bytes 2560 | tf_op jit(solution)/shard_map/scatter | solution.py:91
  17.9 20.2 %all_to_all.10 = s32[2,32,4]{2,0,1:T(2,128)S(1)} all-to-all(s32[2,32,4]{2,0,1:T(2,128)S(1)} %copy.24), channel_id=1, replica_groups=mesh['subj'=8,'space'=32] {'space'}, dimensions={1} | all-to-all | bytes 2048 | tf_op jit(solution)/shard_map/all_to_all | solution.py:93
  38.4 1.2 gather_fusion
  39.7 1.2 copy.29
  40.9 5.8 %all-to-all-start.1 = ((bf16[2,32,4,16,128]{4,3,2,0,1:T(8,128)(2,1)}), bf16[2,32,4,16,128]{4,3,2,0,1:T(8,128)(2,1)}, u32[]{:S(2)}, u32[]{:S(2)}) async-start(bf16[2,32,4,16,128]{4,3,2,0,1:T(8,128)(2,1)} %copy.29), calls=%async_computation.1 | async-start | bytes 2097152 | tf_op jit(solution)/shard_map/all_to_all | solution.py:94
  46.8 13.5 %all_gather.9 = f32[64,16,128]{2,0,1:T(8,128)S(1)} all-gather(f32[64,2,128]{2,0,1:T(8,128)S(1)} %copy.31), channel_id=1, replica_groups=mesh['subj'=8,'space'=32] {'subj'}, dimensions={1}, use_global_device_ids=true | all-gather | bytes 589824 | tf_op jit(solution)/shard_map/all_gather | solution.py:109
  60.3 1.2 copy.32
  61.4 1.6 fusion.52
  64.1 1.7 fusion.51
  65.8 5.9 %all-to-all-done.1 = bf16[2,32,4,16,128]{4,3,2,0,1:T(8,128)(2,1)} async-done(((bf16[2,32,4,16,128]{4,3,2,0,1:T(8,128)(2,1)}), bf16[2,32,4,16,128]{4,3,2,0,1:T(8,128)(2,1)}, u32[]{:S(2)}, u32[]{:S(2)}) %all-to-all-start.1) | async-done | bytes 1048608 | tf_op jit(solution)/shard_map/all_to_all | solution.py:94
  71.8 1.4 copy.30
  76.8 2.3 %fusion.12 = f32[2,64,4,4,128]{4,3,2,1,0:T(4,128)S(1)} fusion(f32[2,64,3,4,128]{4,3,2,1,0:T(4,128)S(1)} %slice.172, f32[2,64,4,4,128]{4,3,2,1,0:T(4,128)S(1)} %bitcast.106, f32[2,64,4,4,127]{4,3,2,1,0:T(4,128)S(1)} %get-tuple-element.35, f32[2,64,4,4,128]{4,3,2,1,0:T(4,128)S(1)} %bitcast.105, f32[2,64,4,4,128]{4,3,2,1,0:T(4,128)S(1)} %bitcast.104, ...), kind=kLoop, calls=%fused_computation.27 | loop fusion | flops 7340032 | bytes 11239936 | tf_op jit(solution)/shard_map/mul | solution.py:107
  82.0 1.9 subtract_divide_fusion.1
  85.0 5.0 %collective-permute-start = (f32[3,2,1,4,4,128]{5,4,3,2,1,0:T(4,128)S(1)}, f32[3,2,1,4,4,128]{5,4,3,2,1,0:T(4,128)S(1)}, u32[]{:S(2)}, u32[]{:S(2)}) collective-permute-start(f32[3,2,1,4,4,128]{5,4,3,2,1,0:T(4,128)S(1)} %get-tuple-element.17), channel_id=1, source_target_pairs={{0,1},{1,2},{2,3},{3,4},{4,5},{5,6},{6,7},{7,8},{8,9},{9,10},{10,1... | collective-permute-start | bytes 147464 | tf_op jit(solution)/shard_map/ppermute | solution.py:17
  90.0 3.1 %collective-permute-start.1 = (f32[3,2,1,4,4,128]{5,4,3,2,1,0:T(4,128)S(1)}, f32[3,2,1,4,4,128]{5,4,3,2,1,0:T(4,128)S(1)}, u32[]{:S(2)}, u32[]{:S(2)}) collective-permute-start(f32[3,2,1,4,4,128]{5,4,3,2,1,0:T(4,128)S(1)} %get-tuple-element.18), channel_id=1, source_target_pairs={{1,0},{2,1},{3,2},{4,3},{5,4},{6,5},{7,6},{8,7},{9,8},{10,9},{11,1... | collective-permute-start | bytes 147464 | tf_op jit(solution)/shard_map/ppermute | solution.py:20
  93.1 2.9 %collective-permute-done.1 = f32[3,2,1,4,4,128]{5,4,3,2,1,0:T(4,128)S(1)} collective-permute-done((f32[3,2,1,4,4,128]{5,4,3,2,1,0:T(4,128)S(1)}, f32[3,2,1,4,4,128]{5,4,3,2,1,0:T(4,128)S(1)}, u32[]{:S(2)}, u32[]{:S(2)}) %collective-permute-start.1) | collective-permute-done | bytes 49184 | tf_op jit(solution)/shard_map/ppermute | solution.py:20
  96.0 2.2 %fusion.5 = f32[3,2,64,4,4,128]{5,4,3,2,1,0:T(4,128)S(1)} fusion(f32[3,2,1,4,4,128]{5,4,3,2,1,0:T(4,128)S(1)} %collective-permute-done.1, f32[3,2,64,4,4,128]{5,4,3,2,1,0:T(4,128)S(1)} %broadcast_multiply_fusion.1, f32[3,2,1,4,4,128]{5,4,3,2,1,0:T(4,128)S(1)} %collective-permute-done), kind=kLoop, calls=%fused_computation.11 | loop fusion | flops 5505024 | bytes 6389760 | tf_op jit(solution)/shard_map/add | solution.py:121
  98.3 2.1 fusion.49
  100.4 4.2 %add_subtract_fusion.1 = f32[3,2,64,4,4,128]{5,4,3,2,1,0:T(4,128)S(1)} fusion(f32[3,2,64,4,4,128]{5,4,3,2,1,0:T(4,128)S(1)} %bitcast.99, f32[3,2,64,4,4,127]{5,4,3,2,1,0:T(4,128)S(1)} %get-tuple-element.16, f32[3,2,64,4,4,127]{5,4,3,2,1,0:T(4,128)S(1)} %get-tuple-element.15, f32[3,2,1,4,4,128]{5,4,3,2,1,0:T(4,128)S(1)} %collective-permute-done.1, ...), kind=kLoop, calls=%fused_computation.17 | loop fusion | flops 10223616 | bytes 15777792 | tf_op jit(solution)/shard_map/sub | solution.py:122
  104.6 3.3 %fusion.45 = (f32[64,4,4,128]{3,2,1,0:T(4,128)}, f32[2,64,4,4,128]{4,3,2,1,0:T(4,128)}) fusion(f32[2,64,4,4,128]{4,3,2,1,0:T(4,128)S(1)} %get-tuple-element.6, f32[3,2,64,4,4,128]{5,4,3,2,1,0:T(4,128)S(1)} %add_subtract_fusion.1, f32[2,64,4,4,128]{4,3,2,1,0:T(4,128)S(1)} %fusion.12, f32[2,64,4,4,128]{4,3,2,1,0:T(4,128)S(1)} %get-tuple-element.5, ...), kind=kLoop, calls=%fused_computation.94 | loop fusion | flops 2228224 | bytes 9437184 | tf_op jit(solution)/shard_map/reduce_sum | solution.py:123
  108.0 33.5 %all-gather.3.cloned.1.call-done = f32[8,64,16,128]{3,2,1,0:T(8,128)} async-done(((f32[1,64,16,128]{3,2,1,0:T(8,128)}), f32[8,64,16,128]{3,2,1,0:T(8,128)}) %all-gather.3.cloned.1.call-update) | async-done | bytes 4194320 | tf_op jit(solution)/shard_map/all_gather | solution.py:125
  141.5 3.3 %reduce_sum.50 = f32[64,16,128]{2,1,0:T(8,128)} reduce(f32[8,64,16,128]{3,2,1,0:T(8,128)} %all-gather.3.cloned.1.call-done, f32[]{:T(128)} %constant.24.clone.1), dimensions={0}, to_apply=%region_4.5 | reduce | flops 917504 | bytes 4718596 | tf_op jit(solution)/shard_map/reduce_sum | solution.py:124
  145.9 2.6 %subtract_divide_fusion = f32[2,64,4,4,128]{4,3,2,1,0:T(4,128)S(1)} fusion(f32[2,64,4,4,128]{4,3,2,1,0:T(4,128)} %get-tuple-element.3, f32[64,4,4,128]{3,2,1,0:T(4,128)S(1)} %bitcast.111, f32[2,64,4,4,128]{4,3,2,1,0:T(4,128)} %copy-done.2, f32[2,64,4,4,128]{4,3,2,1,0:T(4,128)S(1)} %get-tuple-element.5, f32[2,64,3,4,128]{4,3,2,1,0:T(4,128)} %copy-done.6, ...), kind=kLoop, calls=%fused_computation.47 | loop fusion | flops 2621440 | bytes 6291456 | tf_op jit(solution)/shard_map/div | solution.py:116
  149.5 3.5 %collective-permute-start.2 = (f32[3,2,1,4,4,128]{5,4,3,2,1,0:T(4,128)S(1)}, f32[3,2,1,4,4,128]{5,4,3,2,1,0:T(4,128)S(1)}, u32[]{:S(2)}, u32[]{:S(2)}) collective-permute-start(f32[3,2,1,4,4,128]{5,4,3,2,1,0:T(4,128)S(1)} %get-tuple-element.13), channel_id=1, source_target_pairs={{0,1},{1,2},{2,3},{3,4},{4,5},{5,6},{6,7},{7,8},{8,9},{9,10},{10,1... | collective-permute-start | bytes 147464 | tf_op jit(solution)/shard_map/ppermute | solution.py:17
  153.0 4.7 %collective-permute-start.3 = (f32[3,2,1,4,4,128]{5,4,3,2,1,0:T(4,128)S(1)}, f32[3,2,1,4,4,128]{5,4,3,2,1,0:T(4,128)S(1)}, u32[]{:S(2)}, u32[]{:S(2)}) collective-permute-start(f32[3,2,1,4,4,128]{5,4,3,2,1,0:T(4,128)S(1)} %get-tuple-element.14), channel_id=1, source_target_pairs={{1,0},{2,1},{3,2},{4,3},{5,4},{6,5},{7,6},{8,7},{9,8},{10,9},{11,1... | collective-permute-start | bytes 147464 | tf_op jit(solution)/shard_map/ppermute | solution.py:20
  157.7 1.5 collective-permute-done.3
  159.2 2.2 %fusion.1 = f32[3,2,64,4,4,128]{5,4,3,2,1,0:T(4,128)S(1)} fusion(f32[3,2,1,4,4,128]{5,4,3,2,1,0:T(4,128)S(1)} %collective-permute-done.3, f32[3,2,64,4,4,128]{5,4,3,2,1,0:T(4,128)S(1)} %broadcast_multiply_fusion, f32[3,2,1,4,4,128]{5,4,3,2,1,0:T(4,128)S(1)} %collective-permute-done.2), kind=kLoop, calls=%fused_computation.5 | loop fusion | flops 5505024 | bytes 6389760 | tf_op jit(solution)/shard_map/add | solution.py:121
  161.4 2.1 fusion.47
  163.6 4.2 %add_subtract_fusion = f32[3,2,64,4,4,128]{5,4,3,2,1,0:T(4,128)S(1)} fusion(f32[3,2,64,4,4,128]{5,4,3,2,1,0:T(4,128)S(1)} %copy-done.5, f32[3,2,64,4,4,127]{5,4,3,2,1,0:T(4,128)S(1)} %get-tuple-element.12, f32[3,2,64,4,4,127]{5,4,3,2,1,0:T(4,128)S(1)} %get-tuple-element.11, f32[3,2,1,4,4,128]{5,4,3,2,1,0:T(4,128)S(1)} %collective-permute-done.3, ...), kind=kLoop, calls=%fused_computation.16 | loop fusion | flops 10223616 | bytes 15777792 | tf_op jit(solution)/shard_map/sub | solution.py:122
  167.8 2.3 %fusion.15 = f32[64,4,4,128]{3,2,1,0:T(4,128)} fusion(f32[2,64,4,4,128]{4,3,2,1,0:T(4,128)S(1)} %copy-done.3, f32[3,2,64,4,4,128]{5,4,3,2,1,0:T(4,128)S(1)} %add_subtract_fusion, f32[2,64,4,4,128]{4,3,2,1,0:T(4,128)S(1)} %fusion.12, f32[2,64,4,4,128]{4,3,2,1,0:T(4,128)S(1)} %get-tuple-element.5, f32[2,64,3,4,128]{4,3,2,1,0:T(4,128)S(1)} %copy-done.7, ...), kind=kLoop, calls=%fused_computation.31 | loop fusion | flops 2228224 | bytes 8388608 | tf_op jit(solution)/shard_map/reduce_sum | solution.py:123
  170.2 34.7 %all-gather.5.cloned.1.call-done = f32[8,64,16,128]{3,2,1,0:T(8,128)} async-done(((f32[1,64,16,128]{3,2,1,0:T(8,128)}), f32[8,64,16,128]{3,2,1,0:T(8,128)}) %all-gather.5.cloned.1.call-update) | async-done | bytes 4194320 | tf_op jit(solution)/shard_map/all_gather | solution.py:125
  204.9 2.5 %reduce_sum.52 = f32[64,16,128]{2,1,0:T(8,128)S(1)} reduce(f32[8,64,16,128]{3,2,1,0:T(8,128)} %all-gather.5.cloned.1.call-done, f32[]{:T(128)} %constant.24.clone.1), dimensions={0}, to_apply=%region_6.7 | reduce | flops 917504 | bytes 4718596 | tf_op jit(solution)/shard_map/reduce_sum | solution.py:124
  (82 shorter events, 15.9 us)
Async XLA Ops:
  7.2 31.3 %copy-start = (bf16[2,64,16,128]{3,2,1,0:T(8,128)(2,1)S(1)}, bf16[2,64,16,128]{3,2,1,0:T(8,128)(2,1)}, u32[]{:S(2)}) copy-start(bf16[2,64,16,128]{3,2,1,0:T(8,128)(2,1)} %param.7) | copy-start | bytes 1572868
  38.4 8.4 %copy-start.20 = (f32[64,2,128]{2,1,0:T(2,128)S(1)}, f32[64,2,128]{2,1,0:T(2,128)}, u32[]{:S(2)}) copy-start(f32[64,2,128]{2,1,0:T(2,128)} %param.10) | copy-start | bytes 196612
  39.7 21.8 %copy-start.13 = (bf16[3,2,64,16,128]{4,3,2,1,0:T(8,128)(2,1)S(1)}, bf16[3,2,64,16,128]{4,3,2,1,0:T(8,128)(2,1)}, u32[]{:S(2)}) copy-start(bf16[3,2,64,16,128]{4,3,2,1,0:T(8,128)(2,1)} %param.9) | copy-start | bytes 4718596
  40.9 30.8 %all-to-all-start.1 = ((bf16[2,32,4,16,128]{4,3,2,0,1:T(8,128)(2,1)}), bf16[2,32,4,16,128]{4,3,2,0,1:T(8,128)(2,1)}, u32[]{:S(2)}, u32[]{:S(2)}) async-start(bf16[2,32,4,16,128]{4,3,2,0,1:T(8,128)(2,1)} %copy.29), calls=%async_computation.1 | async-start | bytes 2097152 | tf_op jit(solution)/shard_map/all_to_all | solution.py:94
  46.7 94.8 %all-gather.3.cloned.1.call-start = ((), (), s32[]{:S(2)}) async-start(), calls=%async_computation.2 | async-start | bytes 4718592 | tf_op jit(solution)/shard_map/all_gather | solution.py:125
  61.4 2.6 %copy-start.8 = (f32[3,2,64,16,128]{4,3,2,1,0:T(8,128)S(1)}, f32[3,2,64,16,128]{4,3,2,1,0:T(8,128)}, u32[]{:S(2)}) copy-start(f32[3,2,64,16,128]{4,3,2,1,0:T(8,128)} %param.8) | copy-start | bytes 9437188
  75.1 1.6 copy-start.17
  75.1 1.6 copy-start.18
  79.7 1.2 copy-start.14
  79.7 1.5 copy-start.15
  79.8 2.1 copy-start.16
  79.8 2.2 %copy-start.19 = (f32[64,4,4,128]{3,2,1,0:T(4,128)S(1)}, f32[64,4,4,128]{3,2,1,0:T(4,128)}, u32[]{:S(2)}) copy-start(f32[64,4,4,128]{3,2,1,0:T(4,128)} %copy.32) | copy-start | bytes 1572868
  80.5 24.1 %copy-start.6 = (f32[2,64,3,4,128]{4,3,2,1,0:T(4,128)}, f32[2,64,3,4,128]{4,3,2,1,0:T(4,128)S(1)}, u32[]{:S(2)}) copy-start(f32[2,64,3,4,128]{4,3,2,1,0:T(4,128)S(1)} %get-tuple-element.31) | copy-start | bytes 2359300
  84.0 1.0 copy-start.11
  84.0 20.6 %copy-start.2 = (f32[2,64,4,4,128]{4,3,2,1,0:T(4,128)}, f32[2,64,4,4,128]{4,3,2,1,0:T(4,128)S(1)}, u32[]{:S(2)}) copy-start(f32[2,64,4,4,128]{4,3,2,1,0:T(4,128)S(1)} %get-tuple-element.6) | copy-start | bytes 3145732
  85.0 8.1 %collective-permute-start = (f32[3,2,1,4,4,128]{5,4,3,2,1,0:T(4,128)S(1)}, f32[3,2,1,4,4,128]{5,4,3,2,1,0:T(4,128)S(1)}, u32[]{:S(2)}, u32[]{:S(2)}) collective-permute-start(f32[3,2,1,4,4,128]{5,4,3,2,1,0:T(4,128)S(1)} %get-tuple-element.17), channel_id=1, source_target_pairs={{0,1},{1,2},{2,3},{3,4},{4,5},{5,6},{6,7},{7,8},{8,9},{9,10},{10,1... | collective-permute-start | bytes 147464 | tf_op jit(solution)/shard_map/ppermute | solution.py:17
  90.0 6.0 %collective-permute-start.1 = (f32[3,2,1,4,4,128]{5,4,3,2,1,0:T(4,128)S(1)}, f32[3,2,1,4,4,128]{5,4,3,2,1,0:T(4,128)S(1)}, u32[]{:S(2)}, u32[]{:S(2)}) collective-permute-start(f32[3,2,1,4,4,128]{5,4,3,2,1,0:T(4,128)S(1)} %get-tuple-element.18), channel_id=1, source_target_pairs={{1,0},{2,1},{3,2},{4,3},{5,4},{6,5},{7,6},{8,7},{9,8},{10,9},{11,1... | collective-permute-start | bytes 147464 | tf_op jit(solution)/shard_map/ppermute | solution.py:20
  98.3 2.2 %copy-start.9 = (f32[3,2,64,16,128]{4,3,2,1,0:T(8,128)S(1)}, f32[3,2,64,16,128]{4,3,2,1,0:T(8,128)}, u32[]{:S(2)}) copy-start(f32[3,2,64,16,128]{4,3,2,1,0:T(8,128)} %param.8) | copy-start | bytes 9437188
  104.6 3.3 %copy-start.4 = (f32[3,2,64,4,4,128]{5,4,3,2,1,0:T(4,128)}, f32[3,2,64,4,4,128]{5,4,3,2,1,0:T(4,128)S(1)}, u32[]{:S(2)}) copy-start(f32[3,2,64,4,4,128]{5,4,3,2,1,0:T(4,128)S(1)} %add_subtract_fusion.1) | copy-start | bytes 9437188
  108.0 96.9 %all-gather.5.cloned.1.call-start = ((), (), s32[]{:S(2)}) async-start(), calls=%async_computation.3 | async-start | bytes 4718592 | tf_op jit(solution)/shard_map/all_gather | solution.py:125
  145.9 2.7 %copy-start.3 = (f32[2,64,4,4,128]{4,3,2,1,0:T(4,128)S(1)}, f32[2,64,4,4,128]{4,3,2,1,0:T(4,128)}, u32[]{:S(2)}) copy-start(f32[2,64,4,4,128]{4,3,2,1,0:T(4,128)} %copy-done.2) | copy-start | bytes 3145732
  145.9 2.7 %copy-start.12 = (f32[1,2,64,4,4,128]{5,4,3,2,1,0:T(4,128)S(1)}, f32[1,2,64,4,4,128]{5,4,3,2,1,0:T(4,128)}, u32[]{:S(2)}) copy-start(f32[1,2,64,4,4,128]{5,4,3,2,1,0:T(4,128)} %copy-done.11) | copy-start | bytes 3145732
  149.5 8.2 %collective-permute-start.2 = (f32[3,2,1,4,4,128]{5,4,3,2,1,0:T(4,128)S(1)}, f32[3,2,1,4,4,128]{5,4,3,2,1,0:T(4,128)S(1)}, u32[]{:S(2)}, u32[]{:S(2)}) collective-permute-start(f32[3,2,1,4,4,128]{5,4,3,2,1,0:T(4,128)S(1)} %get-tuple-element.13), channel_id=1, source_target_pairs={{0,1},{1,2},{2,3},{3,4},{4,5},{5,6},{6,7},{7,8},{8,9},{9,10},{10,1... | collective-permute-start | bytes 147464 | tf_op jit(solution)/shard_map/ppermute | solution.py:17
  153.0 6.2 %collective-permute-start.3 = (f32[3,2,1,4,4,128]{5,4,3,2,1,0:T(4,128)S(1)}, f32[3,2,1,4,4,128]{5,4,3,2,1,0:T(4,128)S(1)}, u32[]{:S(2)}, u32[]{:S(2)}) collective-permute-start(f32[3,2,1,4,4,128]{5,4,3,2,1,0:T(4,128)S(1)} %get-tuple-element.14), channel_id=1, source_target_pairs={{1,0},{2,1},{3,2},{4,3},{5,4},{6,5},{7,6},{8,7},{9,8},{10,9},{11,1... | collective-permute-start | bytes 147464 | tf_op jit(solution)/shard_map/ppermute | solution.py:20
  161.4 2.2 %copy-start.5 = (f32[3,2,64,4,4,128]{5,4,3,2,1,0:T(4,128)S(1)}, f32[3,2,64,4,4,128]{5,4,3,2,1,0:T(4,128)}, u32[]{:S(2)}) copy-start(f32[3,2,64,4,4,128]{5,4,3,2,1,0:T(4,128)} %copy-done.4) | copy-start | bytes 9437188
  163.6 4.2 %copy-start.7 = (f32[2,64,3,4,128]{4,3,2,1,0:T(4,128)S(1)}, f32[2,64,3,4,128]{4,3,2,1,0:T(4,128)}, u32[]{:S(2)}) copy-start(f32[2,64,3,4,128]{4,3,2,1,0:T(4,128)} %copy-done.6) | copy-start | bytes 2359300
  167.8 2.3 %copy-start.10 = (f32[3,2,64,4,4,128]{5,4,3,2,1,0:T(4,128)}, f32[3,2,64,4,4,128]{5,4,3,2,1,0:T(4,128)S(1)}, u32[]{:S(2)}) copy-start(f32[3,2,64,4,4,128]{5,4,3,2,1,0:T(4,128)S(1)} %add_subtract_fusion) | copy-start | bytes 9437188
  167.8 40.2 %copy-start.1 = (bf16[2,64,16,128]{3,2,1,0:T(8,128)(2,1)S(1)}, bf16[2,64,16,128]{3,2,1,0:T(8,128)(2,1)}, u32[]{:S(2)}) copy-start(bf16[2,64,16,128]{3,2,1,0:T(8,128)(2,1)} %param.7) | copy-start | bytes 1572868
Sparse Core Ops, SparseCore 0:
  108.1 33.3 all-gather.2
  170.3 34.5 all-gather.4
